TPU v7x, 512 devices: a whole 4x8x8 slice. The times are simulated.
512 devices in a mesh: traj: 16 (over z, core), space: 32 (over y, x).
Axes of the slice: x: 4, y: 8, z: 8, core: 2. Of those that a mesh axis runs over, the one named last changes fastest.
Arguments:
- base_state: float32 [256, 1024], P('space'), may hold values from -3 to 3
- perturbations: float32 [16, 16, 256, 1024], P('traj', None, 'space'), may hold values from -2 to 2
- sketch: float32 [256, 16], replicated, may hold values from -0.375 to 0.375
Outputs:
- basis: float32 [16, 256, 1024], P(None, 'space')
All inputs are finite; a program needn't handle non-finite values.
Results may differ from a plain program's by a relative error of at most 0.00027.
Values sent between devices are 32-bit elements; how exact they have to be, the bound alone decides.
A program may use at most 64 MiB of HBM per device.

v0:
```python
import jax
import jax.numpy as jnp
from jax import lax
from jax.sharding import Mesh
from jax.sharding import PartitionSpec as P

STEPS = 4
TRAJ = ("traj_0", "traj_1")


diffusion = 0.4
advection = 0.5
time_step = 0.5


def padded_2(block, sides, width):
    for axis, dim in sides:
        count = lax.axis_size(axis)
        forward = [(i, i + 1) for i in range(count - 1)]
        backward = [(target, source) for source, target in forward]
        low = lax.ppermute(
            lax.slice_in_dim(block, block.shape[dim] - width, None, axis=dim), axis, forward
        )
        high = lax.ppermute(lax.slice_in_dim(block, 0, width, axis=dim), axis, backward)
        block = jnp.concatenate([low, block, high], axis=dim)
    return block


def cut_along(shard, dim, devices):
    before, after = (shard.shape[:dim], shard.shape[dim + 1 :])
    return jnp.moveaxis(shard.reshape(*before, devices, -1, *after), dim, 0)


def sum_at_owner(shard, axis, dim):
    devices = lax.axis_size(axis)
    blocks = lax.all_to_all(cut_along(shard, dim, devices), axis, 0, 0, tiled=True)
    return jnp.sum(blocks, axis=0)


def sum_in_two_steps(shard, axes, dim):
    far, near = axes
    blocks = cut_along(shard, dim, lax.axis_size(far))
    nearer = sum_at_owner(blocks, near, dim + 1)
    arrived = lax.all_to_all(nearer, far, split_axis=0, concat_axis=0, tiled=True)
    return arrived.sum(axis=0)


def filled_up(lines, devices):
    spare = -lines.shape[0] % devices
    if not spare:
        return lines
    return jnp.concatenate([lines, jnp.zeros((spare, *lines.shape[1:]), lines.dtype)])


def from_everyone(shard, axis):
    copies = jnp.broadcast_to(shard, (lax.axis_size(axis), *shard.shape))
    return lax.all_to_all(copies, axis, split_axis=0, concat_axis=0, tiled=True)


def in_order(blocks, dim):
    blocks = jnp.moveaxis(blocks, 0, dim)
    lengths = blocks.shape
    return blocks.reshape(*lengths[:dim], lengths[dim] * lengths[dim + 1], *lengths[dim + 2 :])


def gather_axes(shard, axes, dim):
    far, near = axes
    blocks = from_everyone(from_everyone(shard, far), near)
    return in_order(blocks.swapaxes(0, 1).reshape(-1, *shard.shape), dim)


def nested_sum(shard, axes):
    lines = shard.reshape(-1, shard.shape[-1])
    own = sum_in_two_steps(
        filled_up(lines, lax.axis_size(axes[0]) * lax.axis_size(axes[1])), axes, 0
    )
    whole = gather_axes(own, axes, 0)
    return whole[: len(lines)].reshape(shard.shape)


def of_everyone(shard, axis):
    return from_everyone(shard, axis).sum(axis=0)


def tendency(field):
    center = field[:, 1:-1, :]
    above_row = field[:, 2:, :]
    below_row = field[:, :-2, :]
    east_side = jnp.roll(center, -1, axis=2)
    west_side = jnp.roll(center, 1, axis=2)
    lap_term = above_row + below_row + east_side + west_side - 4.0 * center
    slope = east_side - west_side + (above_row - below_row)
    return diffusion * lap_term - 0.5 * advection * center * slope


def margin_step(fields):
    rows = fields.shape[1]
    padded = padded_2(fields, (("space", 1),), 3)
    first_row = lax.axis_index("space") * rows - 3
    global_rows = first_row + jnp.arange(rows + 6, dtype=jnp.int32)
    inside = ((global_rows >= 0) & (global_rows < lax.axis_size("space") * rows)).astype(
        jnp.float32
    )[None, :, None]
    section_one = (padded[:, 1:-1] + time_step * tendency(padded)) * inside[:, 1:-1]
    section_two = (
        0.75 * padded[:, 2:-2] + 0.25 * (section_one[:, 1:-1] + time_step * tendency(section_one))
    ) * inside[:, 2:-2]
    return padded[:, 3:-3] * (1.0 / 3.0) + 2.0 / 3.0 * (
        section_two[:, 1:-1] + time_step * tendency(section_two)
    )


def row_step(fields):
    return margin_step(fields)


def body(base_state, perturbations, sketch):
    highest = lax.Precision.HIGHEST
    pert_count = perturbations.shape[1]
    rows = base_state.shape[0]
    width = base_state.shape[1]
    devices = lax.axis_size("space")
    cells = devices * rows * width
    fields = jnp.concatenate([base_state[None], base_state[None] + perturbations[0]], axis=0)
    for repeat in range(STEPS):
        fields = row_step(fields)
    snaps = (fields[1:] - fields[0][None]).reshape(pert_count, rows * width)
    own_sketch = lax.dynamic_slice_in_dim(sketch, lax.axis_index(TRAJ) * pert_count, pert_count, 0)
    sketched = lax.dot_general(
        own_sketch,
        snaps,
        (((0,), (0,)), ((), ())),
        precision=highest,
        preferred_element_type=jnp.float32,
    )
    sketched = nested_sum(sketched, ("traj_0", "traj_1"))
    weight_part = lax.dot_general(
        snaps,
        sketched,
        (((1,), (1,)), ((), ())),
        precision=highest,
        preferred_element_type=jnp.float32,
    )
    weights = of_everyone(weight_part, "space") / cells
    proj_part = lax.dot_general(
        weights,
        snaps,
        (((0,), (0,)), ((), ())),
        precision=highest,
        preferred_element_type=jnp.float32,
    )
    projected = nested_sum(proj_part, ("traj_0", "traj_1"))
    small_part = lax.dot_general(
        projected,
        projected,
        (((1,), (1,)), ((), ())),
        precision=highest,
        preferred_element_type=jnp.float32,
    )
    small_gram = of_everyone(small_part, "space") / cells
    lower = jnp.linalg.cholesky(small_gram)
    basis = lax.linalg.triangular_solve(lower, projected, left_side=True, lower=True)
    return basis.reshape(basis.shape[0], rows, width)


def solution(mesh):
    torus = Mesh(mesh.devices.reshape(8, 2, mesh.shape["space"]), ("traj_0", "traj_1", "space"))
    return jax.shard_map(
        body,
        mesh=torus,
        in_specs=(P("space", None), P(TRAJ, None, "space", None), P()),
        out_specs=P(None, "space", None),
        check_vma=False,
    )
```

profile of v0, /device:TPU:1, one launch (start us, length us, event | category | flops | bytes accessed | tf_op | source)
XLA Modules:
  0.0 207.0 jit_solution(2406238697858430054)
XLA Ops:
  0.0 1.1 bitcast_add_fusion
  1.1 1.0 fusion.13
  2.1 4.0 %collective-permute-start = (f32[17,3,1024]{2,1,0:T(4,128)S(1)}, f32[17,3,1024]{2,1,0:T(4,128)S(1)}, u32[]{:S(2)}, u32[]{:S(2)}) collective-permute-start(f32[17,3,1024]{2,1,0:T(4,128)S(1)} %get-tuple-element.59), channel_id=1, source_target_pairs={{0,1},{1,2},{2,3},{3,4},{4,5},{5,6},{6,7},{7,8},{8,9},{9,10},{10,1... | collective-permute-start | bytes 626696 | tf_op jit(solution)/shard_map/ppermute | solution.py:21
  6.0 1.3 collective-permute-start.1
  7.5 2.0 collective-permute-done
  9.5 3.8 %collective-permute-done.1 = f32[17,3,1024]{2,1,0:T(4,128)S(1)} collective-permute-done((f32[17,3,1024]{2,1,0:T(4,128)S(1)}, f32[17,3,1024]{2,1,0:T(4,128)S(1)}, u32[]{:S(2)}, u32[]{:S(2)}) %collective-permute-start.1) | collective-permute-done | bytes 208928 | tf_op jit(solution)/shard_map/ppermute | solution.py:24
  14.2 0.9 add_multiply_fusion.3
  15.6 1.1 fusion.7
  17.6 5.0 %collective-permute-start.2 = (f32[17,3,1024]{2,1,0:T(4,128)S(1)}, f32[17,3,1024]{2,1,0:T(4,128)S(1)}, u32[]{:S(2)}, u32[]{:S(2)}) collective-permute-start(f32[17,3,1024]{2,1,0:T(4,128)S(1)} %get-tuple-element.57), channel_id=1, source_target_pairs={{0,1},{1,2},{2,3},{3,4},{4,5},{5,6},{6,7},{7,8},{8,9},{9,10},{10,1... | collective-permute-start | bytes 626696 | tf_op jit(solution)/shard_map/ppermute | solution.py:21
  22.6 1.3 collective-permute-start.3
  23.9 2.9 %collective-permute-done.2 = f32[17,3,1024]{2,1,0:T(4,128)S(1)} collective-permute-done((f32[17,3,1024]{2,1,0:T(4,128)S(1)}, f32[17,3,1024]{2,1,0:T(4,128)S(1)}, u32[]{:S(2)}, u32[]{:S(2)}) %collective-permute-start.2) | collective-permute-done | bytes 208928 | tf_op jit(solution)/shard_map/ppermute | solution.py:21
  26.8 3.8 %collective-permute-done.3 = f32[17,3,1024]{2,1,0:T(4,128)S(1)} collective-permute-done((f32[17,3,1024]{2,1,0:T(4,128)S(1)}, f32[17,3,1024]{2,1,0:T(4,128)S(1)}, u32[]{:S(2)}, u32[]{:S(2)}) %collective-permute-start.3) | collective-permute-done | bytes 208928 | tf_op jit(solution)/shard_map/ppermute | solution.py:24
  31.5 0.9 add_multiply_fusion.2
  32.9 1.1 fusion.5
  35.0 5.0 %collective-permute-start.4 = (f32[17,3,1024]{2,1,0:T(4,128)S(1)}, f32[17,3,1024]{2,1,0:T(4,128)S(1)}, u32[]{:S(2)}, u32[]{:S(2)}) collective-permute-start(f32[17,3,1024]{2,1,0:T(4,128)S(1)} %get-tuple-element.55), channel_id=1, source_target_pairs={{0,1},{1,2},{2,3},{3,4},{4,5},{5,6},{6,7},{7,8},{8,9},{9,10},{10,1... | collective-permute-start | bytes 626696 | tf_op jit(solution)/shard_map/ppermute | solution.py:21
  39.9 1.5 collective-permute-start.5
  41.4 2.0 collective-permute-done.4
  43.4 3.8 %collective-permute-done.5 = f32[17,3,1024]{2,1,0:T(4,128)S(1)} collective-permute-done((f32[17,3,1024]{2,1,0:T(4,128)S(1)}, f32[17,3,1024]{2,1,0:T(4,128)S(1)}, u32[]{:S(2)}, u32[]{:S(2)}) %collective-permute-start.5) | collective-permute-done | bytes 208928 | tf_op jit(solution)/shard_map/ppermute | solution.py:24
  48.0 0.9 add_multiply_fusion.1
  49.5 1.1 fusion.3
  51.5 4.0 %collective-permute-start.6 = (f32[17,3,1024]{2,1,0:T(4,128)S(1)}, f32[17,3,1024]{2,1,0:T(4,128)S(1)}, u32[]{:S(2)}, u32[]{:S(2)}) collective-permute-start(f32[17,3,1024]{2,1,0:T(4,128)S(1)} %get-tuple-element.53), channel_id=1, source_target_pairs={{0,1},{1,2},{2,3},{3,4},{4,5},{5,6},{6,7},{7,8},{8,9},{9,10},{10,1... | collective-permute-start | bytes 626696 | tf_op jit(solution)/shard_map/ppermute | solution.py:21
  55.6 1.3 collective-permute-start.7
  57.0 2.1 collective-permute-done.6
  59.0 3.8 %collective-permute-done.7 = f32[17,3,1024]{2,1,0:T(4,128)S(1)} collective-permute-done((f32[17,3,1024]{2,1,0:T(4,128)S(1)}, f32[17,3,1024]{2,1,0:T(4,128)S(1)}, u32[]{:S(2)}, u32[]{:S(2)}) %collective-permute-start.7) | collective-permute-done | bytes 208928 | tf_op jit(solution)/shard_map/ppermute | solution.py:24
  63.7 0.9 add_multiply_fusion
  65.1 1.1 fusion.1
  67.8 9.0 %all_to_all.56 = f32[2,8,1,8192]{3,1,2,0:T(8,128)S(1)} all-to-all(f32[2,8,1,8192]{3,1,2,0:T(8,128)S(1)} %convolution_bitcast_fusion.1), channel_id=1, replica_groups=mesh['traj_0'=8,'traj_1'=2,'space'=32] {'traj_1'}, dimensions={0} | all-to-all | bytes 1048576 | tf_op jit(solution)/shard_map/all_to_all | solution.py:36
  77.0 20.9 %all_to_all.57 = f32[8,1,8192]{2,1,0:T(1,128)S(1)} all-to-all(f32[8,1,8192]{2,1,0:T(1,128)S(1)} %reduce_sum.61), channel_id=1, replica_groups=mesh['traj_0'=8,'traj_1'=2,'space'=32] {'traj_0'}, dimensions={0} | all-to-all | bytes 524288 | tf_op jit(solution)/shard_map/all_to_all | solution.py:44
  98.1 0.8 broadcast_in_dim.29
  99.0 3.4 %all-to-all-start.2 = ((f32[8,1,8192]{2,1,0:T(1,128)}), f32[8,1,8192]{2,1,0:T(1,128)S(1)}, u32[]{:S(2)}, u32[]{:S(2)}) async-start(f32[8,1,8192]{2,1,0:T(1,128)} %broadcast_in_dim.29), calls=%async_computation.2 | async-start | bytes 524288 | tf_op jit(solution)/shard_map/all_to_all | solution.py:57
  102.7 9.4 %all-to-all-done.2 = f32[8,1,8192]{2,1,0:T(1,128)S(1)} async-done(((f32[8,1,8192]{2,1,0:T(1,128)}), f32[8,1,8192]{2,1,0:T(1,128)S(1)}, u32[]{:S(2)}, u32[]{:S(2)}) %all-to-all-start.2) | async-done | bytes 262176 | tf_op jit(solution)/shard_map/all_to_all | solution.py:57
  112.3 6.9 %all_to_all.58 = f32[2,8,1,8192]{3,1,2,0:T(8,128)S(1)} all-to-all(f32[2,8,1,8192]{3,1,2,0:T(8,128)S(1)} %broadcast_in_dim.30), channel_id=1, replica_groups=mesh['traj_0'=8,'traj_1'=2,'space'=32] {'traj_1'}, dimensions={0} | all-to-all | bytes 1048576 | tf_op jit(solution)/shard_map/all_to_all | solution.py:57
  120.0 0.8 fusion.47
  121.0 23.8 %all_to_all.59 = f32[32,1,256]{2,1,0:T(1,128)S(1)} all-to-all(f32[32,1,256]{2,1,0:T(1,128)S(1)} %reshape.58), channel_id=1, replica_groups=mesh['traj_0'=8,'traj_1'=2,'space'=32] {'space'}, dimensions={0} | all-to-all | bytes 65536 | tf_op jit(solution)/shard_map/all_to_all | solution.py:57
  145.3 0.7 reduce.10
  146.8 5.4 %all_to_all.60 = f32[2,8,1,8192]{3,1,2,0:T(8,128)S(1)} all-to-all(f32[2,8,1,8192]{3,1,2,0:T(8,128)S(1)} %convolution_bitcast_fusion), channel_id=1, replica_groups=mesh['traj_0'=8,'traj_1'=2,'space'=32] {'traj_1'}, dimensions={0} | all-to-all | bytes 1048576 | tf_op jit(solution)/shard_map/all_to_all | solution.py:36
  152.5 14.7 %all_to_all.61 = f32[8,1,8192]{2,1,0:T(1,128)S(1)} all-to-all(f32[8,1,8192]{2,1,0:T(1,128)S(1)} %reduce_sum.65), channel_id=1, replica_groups=mesh['traj_0'=8,'traj_1'=2,'space'=32] {'traj_0'}, dimensions={0} | all-to-all | bytes 524288 | tf_op jit(solution)/shard_map/all_to_all | solution.py:44
  167.6 14.2 %all_to_all.62 = f32[8,1,8192]{2,1,0:T(1,128)S(1)} all-to-all(f32[8,1,8192]{2,1,0:T(1,128)S(1)} %broadcast_in_dim.32), channel_id=1, replica_groups=mesh['traj_0'=8,'traj_1'=2,'space'=32] {'traj_0'}, dimensions={0} | all-to-all | bytes 524288 | tf_op jit(solution)/shard_map/all_to_all | solution.py:57
  182.0 4.8 %all_to_all.63 = f32[2,8,1,8192]{3,1,2,0:T(8,128)S(1)} all-to-all(f32[2,8,1,8192]{3,1,2,0:T(8,128)S(1)} %broadcast_in_dim.33), channel_id=1, replica_groups=mesh['traj_0'=8,'traj_1'=2,'space'=32] {'traj_1'}, dimensions={0} | all-to-all | bytes 1048576 | tf_op jit(solution)/shard_map/all_to_all | solution.py:57
  187.6 0.8 fusion.48
  188.6 11.7 %all_to_all.64 = f32[32,1,256]{2,1,0:T(1,128)S(1)} all-to-all(f32[32,1,256]{2,1,0:T(1,128)S(1)} %reshape.60), channel_id=1, replica_groups=mesh['traj_0'=8,'traj_1'=2,'space'=32] {'space'}, dimensions={0} | all-to-all | bytes 65536 | tf_op jit(solution)/shard_map/all_to_all | solution.py:57
  200.3 0.7 reduce.11
  201.3 1.5 cholesky.16
  202.7 0.6 compare_reduce_fusion
  203.4 0.6 fusion.15
  204.0 1.2 custom-call.6
  205.3 0.6 fusion.10
  205.9 1.1 copy.46
  (78 shorter events, 15.2 us)
Async XLA Ops:
  0.0 56.9 %copy-start = (f32[256,16]{0,1:T(8,128)S(1)}, f32[256,16]{0,1:T(8,128)}, u32[]{:S(2)}) copy-start(f32[256,16]{0,1:T(8,128)} %param.5) | copy-start | bytes 49156
  0.0 13.3 %copy-start.1 = (f32[8,1024]{1,0:T(8,128)S(1)}, f32[8,1024]{1,0:T(8,128)}, u32[]{:S(2)}) copy-start(f32[8,1024]{1,0:T(8,128)} %param.3) | copy-start | bytes 98308
  2.1 7.4 %collective-permute-start = (f32[17,3,1024]{2,1,0:T(4,128)S(1)}, f32[17,3,1024]{2,1,0:T(4,128)S(1)}, u32[]{:S(2)}, u32[]{:S(2)}) collective-permute-start(f32[17,3,1024]{2,1,0:T(4,128)S(1)} %get-tuple-element.59), channel_id=1, source_target_pairs={{0,1},{1,2},{2,3},{3,4},{4,5},{5,6},{6,7},{7,8},{8,9},{9,10},{10,1... | collective-permute-start | bytes 626696 | tf_op jit(solution)/shard_map/ppermute | solution.py:21
  6.0 7.3 %collective-permute-start.1 = (f32[17,3,1024]{2,1,0:T(4,128)S(1)}, f32[17,3,1024]{2,1,0:T(4,128)S(1)}, u32[]{:S(2)}, u32[]{:S(2)}) collective-permute-start(f32[17,3,1024]{2,1,0:T(4,128)S(1)} %get-tuple-element.60), channel_id=1, source_target_pairs={{1,0},{2,1},{3,2},{4,3},{5,4},{6,5},{7,6},{8,7},{9,8},{10,9},{11,1... | collective-permute-start | bytes 626696 | tf_op jit(solution)/shard_map/ppermute | solution.py:24
  17.6 9.2 %collective-permute-start.2 = (f32[17,3,1024]{2,1,0:T(4,128)S(1)}, f32[17,3,1024]{2,1,0:T(4,128)S(1)}, u32[]{:S(2)}, u32[]{:S(2)}) collective-permute-start(f32[17,3,1024]{2,1,0:T(4,128)S(1)} %get-tuple-element.57), channel_id=1, source_target_pairs={{0,1},{1,2},{2,3},{3,4},{4,5},{5,6},{6,7},{7,8},{8,9},{9,10},{10,1... | collective-permute-start | bytes 626696 | tf_op jit(solution)/shard_map/ppermute | solution.py:21
  22.6 8.0 %collective-permute-start.3 = (f32[17,3,1024]{2,1,0:T(4,128)S(1)}, f32[17,3,1024]{2,1,0:T(4,128)S(1)}, u32[]{:S(2)}, u32[]{:S(2)}) collective-permute-start(f32[17,3,1024]{2,1,0:T(4,128)S(1)} %get-tuple-element.58), channel_id=1, source_target_pairs={{1,0},{2,1},{3,2},{4,3},{5,4},{6,5},{7,6},{8,7},{9,8},{10,9},{11,1... | collective-permute-start | bytes 626696 | tf_op jit(solution)/shard_map/ppermute | solution.py:24
  35.0 8.4 %collective-permute-start.4 = (f32[17,3,1024]{2,1,0:T(4,128)S(1)}, f32[17,3,1024]{2,1,0:T(4,128)S(1)}, u32[]{:S(2)}, u32[]{:S(2)}) collective-permute-start(f32[17,3,1024]{2,1,0:T(4,128)S(1)} %get-tuple-element.55), channel_id=1, source_target_pairs={{0,1},{1,2},{2,3},{3,4},{4,5},{5,6},{6,7},{7,8},{8,9},{9,10},{10,1... | collective-permute-start | bytes 626696 | tf_op jit(solution)/shard_map/ppermute | solution.py:21
  39.9 7.3 %collective-permute-start.5 = (f32[17,3,1024]{2,1,0:T(4,128)S(1)}, f32[17,3,1024]{2,1,0:T(4,128)S(1)}, u32[]{:S(2)}, u32[]{:S(2)}) collective-permute-start(f32[17,3,1024]{2,1,0:T(4,128)S(1)} %get-tuple-element.56), channel_id=1, source_target_pairs={{1,0},{2,1},{3,2},{4,3},{5,4},{6,5},{7,6},{8,7},{9,8},{10,9},{11,1... | collective-permute-start | bytes 626696 | tf_op jit(solution)/shard_map/ppermute | solution.py:24
  51.5 7.5 %collective-permute-start.6 = (f32[17,3,1024]{2,1,0:T(4,128)S(1)}, f32[17,3,1024]{2,1,0:T(4,128)S(1)}, u32[]{:S(2)}, u32[]{:S(2)}) collective-permute-start(f32[17,3,1024]{2,1,0:T(4,128)S(1)} %get-tuple-element.53), channel_id=1, source_target_pairs={{0,1},{1,2},{2,3},{3,4},{4,5},{5,6},{6,7},{7,8},{8,9},{9,10},{10,1... | collective-permute-start | bytes 626696 | tf_op jit(solution)/shard_map/ppermute | solution.py:21
  55.6 7.3 %collective-permute-start.7 = (f32[17,3,1024]{2,1,0:T(4,128)S(1)}, f32[17,3,1024]{2,1,0:T(4,128)S(1)}, u32[]{:S(2)}, u32[]{:S(2)}) collective-permute-start(f32[17,3,1024]{2,1,0:T(4,128)S(1)} %get-tuple-element.54), channel_id=1, source_target_pairs={{1,0},{2,1},{3,2},{4,3},{5,4},{6,5},{7,6},{8,7},{9,8},{10,9},{11,1... | collective-permute-start | bytes 626696 | tf_op jit(solution)/shard_map/ppermute | solution.py:24
  99.0 13.1 %all-to-all-start.2 = ((f32[8,1,8192]{2,1,0:T(1,128)}), f32[8,1,8192]{2,1,0:T(1,128)S(1)}, u32[]{:S(2)}, u32[]{:S(2)}) async-start(f32[8,1,8192]{2,1,0:T(1,128)} %broadcast_in_dim.29), calls=%async_computation.2 | async-start | bytes 524288 | tf_op jit(solution)/shard_map/all_to_all | solution.py:57
where the time goes:
time: 208 us; the launch traced here: 207 us
  blocking collectives  112 us (54%)
  waiting for transfers between devices  33.6 us (16%)
  starting transfers between devices  26.7 us (13%)
  other arithmetic  18.6 us (9%)
  local copies, waits for them, and re-layouts  12.6 us (6%)
  matrix products  3.34 us (2%)
    all_to_all x5, blocking collectives, from_everyone(): return lax.all_to_all(copies, axis, split_axis=0, concat_axis=0, tiled=True)  61.5 us
    all_to_all x2, blocking collectives, sum_in_two_steps(): lax.all_to_all(nearer, far, split_axis=0, concat_axis=0, tiled=True)  35.7 us
    ppermute x4, starting transfers between devices, padded_2(): lax.ppermute(lax.slice_in_dim(block, block.shape[dim] - width, None, axis...  17.9 us
    ppermute x4, waiting for transfers between devices, padded_2(): lax.ppermute(lax.slice_in_dim(block, 0, width, axis=dim), axis, backward)  15.3 us
    all_to_all x2, blocking collectives, sum_at_owner(): lax.all_to_all(cut_along(shard, dim, devices), axis, 0, 0, tiled=True)  14.5 us
    all_to_all x1, waiting for transfers between devices, from_everyone(): return lax.all_to_all(copies, axis, split_axis=0, concat_axis=0, tiled=True)  9.37 us
    ppermute x4, waiting for transfers between devices, padded_2(): lax.ppermute(lax.slice_in_dim(block, block.shape[dim] - width, None, axis...  8.91 us
    slice x24, local copies, waits for them, and re-layouts, tendency(): east_side = jnp.roll(center, -1, axis=2)  5.96 us
  transfers between devices with their start and end apart: 9, of which 9 were waited for; matrix products, arithmetic and copies ran while one was open for 0% of the time, Pallas kernels for 0%

commit v1 on v0

v1 whole, which is shorter than its diff:
```python
import functools

import jax
import jax.numpy as jnp
from jax import lax
from jax.experimental import pallas as pl
from jax.experimental.pallas import tpu as pltpu
from jax.sharding import Mesh
from jax.sharding import PartitionSpec as P

STEPS = 4
CORES = 2
ALONG_X = 4
HALO_TILES = 2
MESH = pl.DeviceIdType.MESH
F32 = jnp.float32


def shifted(c):
    lane = lax.broadcasted_iota(jnp.int32, c.shape, c.ndim - 1)
    a, s = c.ndim - 1, c.ndim - 2
    e = pltpu.roll(c, 127, a)
    e = jnp.where(lane == 127, pltpu.roll(e, 7, s), e)
    w = pltpu.roll(c, 1, a)
    w = jnp.where(lane == 0, pltpu.roll(w, 1, s), w)
    return e, w


def parts_of(lo, hi, first, last):
    cuts = [lo]
    while cuts[-1] < hi:
        at = cuts[-1]
        if at < first:
            at = min(first, hi)
        elif at < last:
            at = min(at + 8, last)
        else:
            at = hi
        cuts.append(at)
    return list(zip(cuts[:-1], cuts[1:]))


def stage(src, field, dst, lo, hi, first, last, low, high, mix):
    keep, take = mix
    for r0, r1 in parts_of(lo, hi, first, last):
        c = src[r0:r1]
        e, w = shifted(c)
        p = e + src[r0 + 1 : r1 + 1]
        m = w + src[r0 - 1 : r1 - 1]
        out = (0.2 * take) * ((p + m) + c) - ((0.125 * take) * c) * (p - m)
        if keep:
            out = keep * field[r0:r1] + out
        if r1 <= first:
            out = out * low
        elif r0 >= last:
            out = out * high
        dst[r0:r1] = out


def advance(v, w1, w2, first, last, low, high):
    lo, hi = first - 3 * STEPS, last + 3 * STEPS
    for _ in range(STEPS):
        args = (first, last, low, high)
        stage(v, v, w1, lo + 1, hi - 1, *args, (0.0, 1.0))
        stage(w1, v, w2, lo + 2, hi - 2, *args, (0.75, 0.25))
        stage(w2, v, v, lo + 3, hi - 3, *args, (1.0 / 3.0, 2.0 / 3.0))
        lo, hi = lo + 3, hi - 3


def peers_of(dims):
    X, Y, Z, C = dims
    x, y, z, c = (lax.axis_index(n) for n in "xyzc")

    def column(n):
        return {"c": lax.rem(c + lax.rem(n, C), C), "z": lax.rem(z + n // C, Z)}

    def plane(n):
        return {"x": lax.rem(x + lax.rem(n, X), X), "y": lax.rem(y + n // X, Y)}

    return column, plane


def each(count, do):
    def step(n, carry):
        do(n)
        return carry

    lax.fori_loop(1, count, step, 0)


def snapshots_body(dims, base_ref, pert_ref, got, raw, basein, bv, v, w1, w2, fb, send, xs_send, xs_recv, own_sem, y_send, y_recv, a_send, a_recv):
    X, Y, Z, C = dims
    TL = raw.shape[0]
    KB = TL // 2
    NS = X * Z * C
    first, last = 8 * HALO_TILES, 8 * (HALO_TILES + X)
    x, y, z, c = (lax.axis_index(n) for n in "xyzc")
    me = (z * C + c) * X + x
    below, above = y > 0, y < Y - 1
    low = jnp.where(below, 1.0, 0.0).astype(F32)
    high = jnp.where(above, 1.0, 0.0).astype(F32)

    def target(n):
        return {
            "x": lax.rem(x + lax.rem(n // C, X), X),
            "c": lax.rem(c + lax.rem(n, C), C),
            "z": lax.rem(z + n // (C * X), Z),
        }

    barrier = pltpu.get_barrier_semaphore()

    def greet(n, carry):
        pl.semaphore_signal(barrier, inc=1, device_id=target(n), device_id_type=MESH)
        return carry

    lax.fori_loop(1, NS, greet, 0)
    column, plane = peers_of(dims)

    def greet_plane(n, carry):
        pl.semaphore_signal(barrier, inc=1, device_id=plane(n), device_id_type=MESH)
        return carry

    lax.fori_loop(X, X * Y, greet_plane, 0)
    pl.semaphore_wait(barrier, NS - 1 + X * Y - X)

    def x_copy(t, d):
        to = lax.rem(x + d, X)
        source = base_ref if t is None else pert_ref.at[to * TL + t]
        dest = basein.at[HALO_TILES + x] if t is None else raw.at[t, HALO_TILES + x]
        slot = TL if t is None else t
        return pltpu.make_async_remote_copy(
            source, dest, xs_send.at[slot, d], xs_recv.at[slot, d], device_id={"x": to}, device_id_type=MESH
        )

    def own_copy(t):
        source = base_ref if t is None else pert_ref.at[x * TL + t]
        dest = basein.at[HALO_TILES + x] if t is None else raw.at[t, HALO_TILES + x]
        return pltpu.make_async_copy(source, dest, own_sem.at[TL if t is None else t])

    order = [d for d in (1, X - 1, 2) if d < X]
    order = list(dict.fromkeys(order))
    for t in [None, *range(TL)]:
        own_copy(t).start()
        for d in order:
            x_copy(t, d).start()

    def up(t):
        buf = basein if t is None else raw.at[t]
        slot = TL if t is None else t
        return pltpu.make_async_remote_copy(
            buf.at[pl.ds(X, 2)], buf.at[pl.ds(0, 2)], y_send.at[slot, 0], y_recv.at[slot, 0],
            device_id={"y": y + 1}, device_id_type=MESH,
        )

    def down(t):
        buf = basein if t is None else raw.at[t]
        slot = TL if t is None else t
        return pltpu.make_async_remote_copy(
            buf.at[pl.ds(2, 2)], buf.at[pl.ds(X + 2, 2)], y_send.at[slot, 1], y_recv.at[slot, 1],
            device_id={"y": y - 1}, device_id_type=MESH,
        )

    def arrive_x(t):
        own_copy(t).wait()
        for d in order:
            x_copy(t, d).wait_recv()

    def pass_on(t):
        @pl.when(above)
        def _():
            up(t).start()

        @pl.when(below)
        def _():
            down(t).start()

    def arrive_y(t):
        buf = basein if t is None else raw.at[t]

        @pl.when(below)
        def _():
            up(t).wait_recv()

        @pl.when(above)
        def _():
            down(t).wait_recv()

        @pl.when(jnp.logical_not(below))
        def _():
            buf[0:2] = jnp.zeros((2, 64, 128), F32)

        @pl.when(jnp.logical_not(above))
        def _():
            buf[X + 2 : X + 4] = jnp.zeros((2, 64, 128), F32)

    def rows_of(buf, row):
        return buf[row // 8, pl.ds(row % 8, 8, stride=8), :]

    for t in [None, 0, 1]:
        arrive_x(t)
        pass_on(t)
    arrive_y(None)
    for row in range(first - 12, last + 12):
        val = rows_of(basein, row)
        bv[row] = val
        v[row] = val
    advance(v, w1, w2, first, last, low, high)
    for i in range(X):
        fb[8 * i : 8 * i + 8] = v[first + 8 * i : first + 8 * i + 8]

    def out_copy(b, n):
        to = target(n)
        return pltpu.make_async_remote_copy(
            send.at[b, to["x"], to["z"], to["c"]], got.at[b, pl.ds(pl.multiple_of(8 * me, 8), 8)], a_send.at[b], a_recv.at[b],
            device_id=to, device_id_type=MESH,
        )

    def mine(b):
        return pltpu.make_async_copy(send.at[b, x, z, c], got.at[b, pl.ds(pl.multiple_of(8 * me, 8), 8)], a_recv.at[b])

    def pair(b, carry):
        for f in range(2):
            t = 2 * b + f

            @pl.when(t + 2 < TL)
            def _():
                arrive_x(t + 2)
                pass_on(t + 2)

            arrive_y(t)
            for row in range(first - 12, last + 12):
                v[row] = bv[row] + rows_of(raw.at[t], row)
            advance(v, w1, w2, first, last, low, high)
            half = lax.broadcasted_iota(jnp.int32, (8, 8, 128), 1) < 4
            for i in range(X):
                snap = v[first + 8 * i : first + 8 * i + 8] - fb[8 * i : 8 * i + 8]
                turned = pltpu.roll(snap, 4, 1)
                if f == 0:
                    send[b, i, :, 0] = snap
                    send[b, i, :, 1] = turned
                else:
                    send[b, i, :, 0] = jnp.where(half, send[b, i, :, 0], turned)
                    send[b, i, :, 1] = jnp.where(half, send[b, i, :, 1], snap)

        def give(n, carry):
            out_copy(b, n).start()
            return carry

        mine(b).start()
        lax.fori_loop(1, NS, give, 0)
        return carry

    lax.fori_loop(0, KB, pair, 0)


    def finish():
        for t in [None, *range(TL)]:
            for d in order:
                x_copy(t, d).wait_send()

            @pl.when(above)
            def _():
                up(t).wait_send()

            @pl.when(below)
            def _():
                down(t).wait_send()

        for b in range(KB):
            others = got.at[b, pl.ds(0, 8 * NS - 8)]
            pltpu.make_async_copy(others, others, a_send.at[b]).wait()

    return finish


def inverse_factor(gram):
    row = lax.broadcasted_iota(jnp.int32, (16, 128), 0)
    lane = lax.broadcasted_iota(jnp.int32, (16, 128), 1)
    a = jnp.where(lane < 16, gram, jnp.where(lane == row + 16, 1.0, 0.0))
    for k in range(16):
        scale = 1.0 / jnp.sqrt(a[k : k + 1, k : k + 1])
        pivot = a[k : k + 1, :] * scale
        factor = a[:, k : k + 1] * scale
        a = jnp.where(row > k, a - factor * pivot, jnp.where(row == k, pivot, a))
    return a


def reduce_body(dims, omega_ref, out_ref, got, a_recv, S, wsend, wrecv, own, own_row, plane_recv, w_all, psend, pall, small, small_plane, small_column, sems):
    X, Y, Z, C = dims
    KB = got.shape[0]
    TL = 2 * KB
    NZC, NXY, NS = Z * C, X * Y, X * Z * C
    cells = Y * X * 8 * 1024
    x, y, z, c = (lax.axis_index(n) for n in "xyzc")
    mine, here = z * C + c, y * X + x
    column, plane = peers_of(dims)

    def dot(a, b, dims):
        return lax.dot_general(a, b, (dims, ((), ())), precision=lax.Precision.HIGHEST, preferred_element_type=F32)

    for b in range(KB):
        everything = got.at[b]
        pltpu.make_async_copy(everything, everything, a_recv.at[b]).wait()
        for f in range(2):
            for q in range(4):
                S[q, pl.ds(2 * b + f, NS, stride=TL), :] = got[b, pl.ds(4 * f + q, NS, stride=8), :]
    mat = jnp.concatenate([S[q] for q in range(4)], axis=1)
    sketched = dot(omega_ref[...], mat, ((1,), (0,)))
    part = dot(sketched, mat, ((1,), (1,))) * (1.0 / cells)
    for h in range(2):
        wsend[h] = part[:, 128 * h : 128 * h + 128]

    def remote(src, dst, k, n, to):
        return pltpu.make_async_remote_copy(
            src, dst, sems.at[0, k, n], sems.at[1, k, n], device_id=to, device_id_type=MESH
        )

    def scatter(n):
        to = column(n)
        row = to["z"] * C + to["c"]
        return remote(wsend.at[:, pl.ds(row, 1), :], wrecv.at[:, pl.ds(mine, 1), :], 0, n, to)

    def spread(n):
        return remote(own, plane_recv.at[here], 1, n, plane(n))

    def gather(n):
        return remote(own_row.at[:, pl.ds(0, 1), :], w_all.at[:, pl.ds(mine, 1), :], 2, n, column(n))

    def projected(n):
        return remote(psend, pall.at[pl.ds(4 * c, 4), :, z, :], 3, n, column(n))

    def small_spread(n):
        return remote(small.at[0], small_plane.at[here], 4, n, plane(n))

    def small_gather(n):
        return remote(small.at[1], small_column.at[mine], 5, n, column(n))

    each(NZC, lambda n: scatter(n).start())
    wrecv[:, pl.ds(mine, 1), :] = wsend[:, pl.ds(mine, 1), :]
    each(NZC, lambda n: scatter(n).wait_recv())
    value = jnp.sum(wrecv[...], axis=1)
    own[...] = value
    each(NXY, lambda n: spread(n).start())
    plane_recv[here] = value
    each(NXY, lambda n: spread(n).wait_recv())
    value = jnp.sum(plane_recv[...], axis=0)
    for h in range(2):
        own_row[h, 0:1, :] = value[h : h + 1]
    each(NZC, lambda n: gather(n).start())
    for h in range(2):
        w_all[h, pl.ds(mine, 1), :] = value[h : h + 1]
    each(NZC, lambda n: gather(n).wait_recv())
    weights = jnp.concatenate([w_all[0], w_all[1]], axis=1)
    proj = dot(weights, mat, ((1,), (0,)))
    for q in range(4):
        psend[q] = proj[:, 128 * q : 128 * q + 128]
    each(NZC, lambda n: projected(n).start())
    own_p = pltpu.make_async_copy(psend, pall.at[pl.ds(4 * c, 4), :, z, :], sems.at[0, 3, 0])
    own_p.start()

    row = lax.broadcasted_iota(jnp.int32, (16, 128), 0)
    lane = lax.broadcasted_iota(jnp.int32, (16, 128), 1)
    diagonal = lane // 16 == lax.rem(row, 8)
    wide = dot(proj, jnp.concatenate([proj] * 8, axis=0), ((1,), (1,))) * (1.0 / cells)
    wide = jnp.where(diagonal, wide, 0.0)
    value = jnp.concatenate([jnp.sum(wide[8 * h : 8 * h + 8], axis=0, keepdims=True) for h in range(2)], axis=0)
    small[0] = value
    each(NXY, lambda n: small_spread(n).start())
    small_plane[here] = value
    each(NXY, lambda n: small_spread(n).wait_recv())
    value = jnp.sum(small_plane[...], axis=0)
    small[1] = value
    each(NZC, lambda n: small_gather(n).start())
    small_column[mine] = value
    each(NZC, lambda n: small_gather(n).wait_recv())
    value = jnp.sum(small_column[...], axis=0)
    gram = jnp.concatenate([jnp.broadcast_to(value[h : h + 1], (8, 128)) for h in range(2)], axis=0)
    gram = jnp.where(diagonal, gram, 0.0)
    for shift in (64, 32, 16):
        gram = gram + pltpu.roll(gram, shift, 1)
    inverse = inverse_factor(gram)

    own_p.wait()
    each(NZC, lambda n: projected(n).wait_recv())
    for i in range(16):
        total = inverse[i : i + 1, 16:17] * pall[:, 0]
        for m in range(1, i + 1):
            total = total + inverse[i : i + 1, 16 + m : 17 + m] * pall[:, m]
        out_ref[i] = total

    each(NZC, lambda n: scatter(n).wait_send())
    each(NXY, lambda n: spread(n).wait_send())
    each(NZC, lambda n: gather(n).wait_send())
    each(NZC, lambda n: projected(n).wait_send())
    each(NXY, lambda n: small_spread(n).wait_send())
    each(NZC, lambda n: small_gather(n).wait_send())


def whole_body(dims, base_ref, pert_ref, omega_ref, out_ref, *scratch):
    got, one, two = scratch[0], scratch[1:16], scratch[16:]
    finish = snapshots_body(dims, base_ref, pert_ref, got, *one)
    reduce_body(dims, omega_ref, out_ref, got, one[-1], *two)
    finish()


def basis_of(base, pert, omega, dims):
    X, Y, Z, C = dims
    TL = pert.shape[0] // X
    KB, NS, NZC, NXY = TL // 2, X * Z * C, Z * C, X * Y
    rows = 8 * (X + 2 * HALO_TILES)
    sem = pltpu.SemaphoreType.DMA
    anywhere = pl.BlockSpec(memory_space=pl.ANY)
    inside = pl.BlockSpec(memory_space=pltpu.VMEM)
    vmem = lambda *shape: pltpu.VMEM(shape, F32)
    return pl.pallas_call(
        functools.partial(whole_body, dims),
        out_shape=jax.ShapeDtypeStruct((16, 8, 8, 128), F32),
        in_specs=[anywhere, anywhere, inside],
        out_specs=inside,
        scratch_shapes=[
            vmem(KB, NS * 8, 128),
            vmem(TL, rows // 8, 64, 128),
            vmem(rows // 8, 64, 128),
            vmem(rows, 8, 128),
            vmem(rows, 8, 128),
            vmem(rows, 8, 128),
            vmem(rows, 8, 128),
            vmem(8 * X, 8, 128),
            vmem(KB, X, Z, C, 8, 128),
            sem((TL + 1, X)),
            sem((TL + 1, X)),
            sem((TL + 1,)),
            sem((TL + 1, 2)),
            sem((TL + 1, 2)),
            sem((KB,)),
            sem((KB,)),
            vmem(4, NS * TL, 128),
            vmem(2, 16, 128),
            vmem(2, 16, 128),
            vmem(2, 128),
            vmem(2, 8, 128),
            vmem(NXY, 2, 128),
            vmem(2, 16, 128),
            vmem(4, 16, 128),
            vmem(8, 16, 8, 128),
            vmem(2, 2, 128),
            vmem(NXY, 2, 128),
            vmem(NZC, 2, 128),
            sem((2, 6, max(NXY, NZC))),
        ],
        compiler_params=pltpu.CompilerParams(collective_id=0, has_side_effects=True),
    )(base, pert, omega)


def tiles_first(a):
    lead = a.shape[:-2]
    a = a.reshape(*lead, 8, 8, 128)
    n = len(lead)
    return a.transpose(*range(n), n + 1, n, n + 2).reshape(*lead, 64, 128)


def body(dims, base_state, perturbations, sketch):
    out = basis_of(tiles_first(base_state), tiles_first(perturbations[0]), sketch.T, dims)
    return out.transpose(0, 2, 1, 3).reshape(16, 8, 1024)


def solution(mesh, along_x=ALONG_X):
    traj, space = mesh.shape["traj"], mesh.shape["space"]
    dims = (along_x, space // along_x, traj // CORES, CORES)
    X, Y, Z, C = dims
    torus = Mesh(mesh.devices.reshape(Z, C, Y, X), ("z", "c", "y", "x"))
    return jax.shard_map(
        functools.partial(body, dims),
        mesh=torus,
        in_specs=(P(("y", "x"), None), P(("z", "c"), None, ("y", "x"), None), P()),
        out_specs=P(None, ("y", "x"), None),
        check_vma=False,
    )
```

time: 208 us -> 86.9 us (0.42)
  blocking collectives: 112 us -> 0 us
  Pallas kernels: 0 us -> 84.7 us
  waiting for transfers between devices: 33.6 us -> 0 us
  starting transfers between devices: 26.7 us -> 0 us
  other arithmetic: 18.6 us -> 0 us
  local copies, waits for them, and re-layouts: 12.6 us -> 1.89 us
  matrix products: 3.34 us -> 0 us
    all_to_all x9 -> x0, blocking collectives: 112 us -> none  [the longest x5 61.5 us: from_everyone(): return lax.all_to_all(copies, axis, split_axis=0, concat_axis=0, tiled=True)]
    pallas_call x0 -> x1, Pallas kernels: none -> 84.7 us  [basis_of(): pl.pallas_call(functools.partial(whole_body, dims), out_shape=jax.ShapeDt...]
    ppermute x8 -> x0, waiting for transfers between devices: 24.3 us -> none  [the longest x4 15.3 us: padded_2(): lax.ppermute(lax.slice_in_dim(block, 0, width, axis=dim), axis, backward)]
    ppermute x8 -> x0, starting transfers between devices: 23.3 us -> none  [the longest x4 17.9 us: padded_2(): lax.ppermute(lax.slice_in_dim(block, block.shape[dim] - width, None, axis...]
    all_to_all x1 -> x0, waiting for transfers between devices: 9.37 us -> none  [from_everyone(): return lax.all_to_all(copies, axis, split_axis=0, concat_axis=0, tiled=True)]
    mul x8 -> x0, other arithmetic: 7.67 us -> none  [the longest x4 4.2 us: margin_step(): (0.75 * padded[:, 2:-2] + 0.25 * (section_one[:, 1:-1] + time_step * tend...]
    slice x27 -> x0, local copies, waits for them, and re-layouts: 6.33 us -> none  [the longest x24 5.96 us: tendency(): east_side = jnp.roll(center, -1, axis=2)]
    another operation x5 -> x0, other arithmetic: 4.01 us -> none  [the longest x3 2.13 us: body(): lower = jnp.linalg.cholesky(small_gram)]
  transfers between devices with their start and end apart: 9 -> 0, of which waited for: 9 -> 0; matrix products, arithmetic and copies ran while one was open for 0% -> 0% of each run, Pallas kernels for 0% -> 0%
where the time goes in v1:
time: 86.9 us; the launch traced here: 86.6 us
  Pallas kernels  84.7 us (97%)
  local copies, waits for them, and re-layouts  1.89 us (2%)
    pallas_call x1, Pallas kernels, basis_of(): pl.pallas_call(functools.partial(whole_body, dims), out_shape=jax.ShapeDt...  84.7 us
    unnamed x1, local copies, waits for them, and re-layouts  1.89 us

profile of v1, /device:TPU:1, one launch (start us, length us, event | category | flops | bytes accessed | tf_op | source)
XLA Modules:
  0.0 86.6 jit_solution(16524869654636569656)
XLA Ops:
  0.0 84.7 %shard_map.37 = f32[16,8,8,128]{3,2,1,0:T(8,128)} custom-call(f32[64,128]{1,0:T(8,128)} %bitcast.16, f32[16,64,128]{2,1,0:T(8,128)} %bitcast.15, f32[16,256]{1,0:T(8,128)} %bitcast.17), custom_call_target="tpu_custom_call" | custom-call | tf_op jit(solution)/shard_map/pallas_call | solution.py:415
  84.8 1.9 %copy.5 = f32[16,8,1024]{2,1,0:T(8,128)} copy(f32[16,8,1024]{2,1,0:T(8,128)} %bitcast.14) | data formatting | bytes 1048576

commit v2 on v1

v2 whole, which is shorter than its diff:
```python
import functools

import jax
import jax.numpy as jnp
from jax import lax
from jax.experimental import pallas as pl
from jax.experimental.pallas import tpu as pltpu
from jax.sharding import Mesh
from jax.sharding import PartitionSpec as P

STEPS = 4
CORES = 2
ALONG_X = 4
HALO_TILES = 2
MESH = pl.DeviceIdType.MESH
F32 = jnp.float32


def shifted(c):
    lane = lax.broadcasted_iota(jnp.int32, c.shape, c.ndim - 1)
    a, s = c.ndim - 1, c.ndim - 2
    e = pltpu.roll(c, 127, a)
    e = jnp.where(lane == 127, pltpu.roll(e, 7, s), e)
    w = pltpu.roll(c, 1, a)
    w = jnp.where(lane == 0, pltpu.roll(w, 1, s), w)
    return e, w


def parts_of(lo, hi, first, last):
    cuts = [lo]
    while cuts[-1] < hi:
        at = cuts[-1]
        if at < first:
            at = min(first, hi)
        elif at < last:
            at = min(at + 8, last)
        else:
            at = hi
        cuts.append(at)
    return list(zip(cuts[:-1], cuts[1:]))


def stage(src, field, dst, lo, hi, first, last, low, high, mix):
    keep, take = mix
    for r0, r1 in parts_of(lo, hi, first, last):
        c = src[r0:r1]
        e, w = shifted(c)
        p = e + src[r0 + 1 : r1 + 1]
        m = w + src[r0 - 1 : r1 - 1]
        out = (0.2 * take) * ((p + m) + c) - ((0.125 * take) * c) * (p - m)
        if keep:
            out = keep * field[r0:r1] + out
        if r1 <= first:
            out = out * low
        elif r0 >= last:
            out = out * high
        dst[r0:r1] = out


def advance(v, w1, w2, first, last, low, high):
    lo, hi = first - 3 * STEPS, last + 3 * STEPS
    for _ in range(STEPS):
        args = (first, last, low, high)
        stage(v, v, w1, lo + 1, hi - 1, *args, (0.0, 1.0))
        stage(w1, v, w2, lo + 2, hi - 2, *args, (0.75, 0.25))
        stage(w2, v, v, lo + 3, hi - 3, *args, (1.0 / 3.0, 2.0 / 3.0))
        lo, hi = lo + 3, hi - 3


def wrapped(at, size):
    return [at] + [jnp.where(at + d < size, at + d, at + d - size) for d in range(1, size)]


def far_first(size):
    return sorted(range(size), key=lambda d: (-min(d, size - d), d))


def settle(like, sem):
    pltpu.make_async_copy(like, like, sem).wait()


class Places:
    def __init__(self, dims):
        X, Y, Z, C = self.dims = dims
        self.x, self.y, self.z, self.c = (lax.axis_index(n) for n in "xyzc")
        self.xs, self.ys = wrapped(self.x, X), wrapped(self.y, Y)
        self.zs, self.cs = wrapped(self.z, Z), wrapped(self.c, C)
        self.column = [(dz, dc) for dz in far_first(Z) for dc in range(C) if dz or dc]
        self.plane = sorted(
            ((dy, dx) for dy in range(Y) for dx in range(X) if dy or dx),
            key=lambda d: -min(d[0], Y - d[0]) - min(d[1], X - d[1]),
        )
        self.all = sorted(
            ((dz, dc, dx) for dz in range(Z) for dc in range(C) for dx in range(X) if dz or dc or dx),
            key=lambda d: -min(d[0], Z - d[0]) - min(d[2], X - d[2]),
        )


def snapshots_body(at, base_ref, pert_ref, got, pertv, basev, raw, v, w1, w2, send, in_sem, hello, xs_send, xs_recv, y_send, y_recv, a_send, a_recv):
    X, Y, Z, C = at.dims
    TL = raw.shape[0] - 1
    NS = X * Z * C
    first, last = 8 * HALO_TILES, 8 * (HALO_TILES + X)
    x, y, z, c = at.x, at.y, at.z, at.c
    me = (z * C + c) * X + x
    below, above = y > 0, y < Y - 1
    low = jnp.where(below, 1.0, 0.0).astype(F32)
    high = jnp.where(above, 1.0, 0.0).astype(F32)
    order = far_first(X)[:-1]
    rounds = max(Z, Y) // 2

    def signal(sem, to):
        pl.semaphore_signal(sem, inc=1, device_id=to, device_id_type=MESH)

    barrier = pltpu.get_barrier_semaphore()
    for dx in range(X):
        for dc in range(C):
            if dx or dc:
                signal(barrier, {"x": at.xs[dx], "c": at.cs[dc]})
    around = [{"z": at.zs[1]}, {"z": at.zs[Z - 1]}, {"y": at.ys[1]}, {"y": at.ys[Y - 1]}]
    for to in around:
        signal(barrier, to)

    base_in = pltpu.make_async_copy(base_ref, basev, in_sem.at[0])
    pert_in = pltpu.make_async_copy(pert_ref, pertv, in_sem.at[1])
    base_in.start()
    pert_in.start()
    base_in.wait()
    pert_in.wait()
    for k in range(X * TL):
        pertv[k] = pertv[k] + basev[...]
    pl.semaphore_wait(barrier, X * C - 1 + 4)

    def greet(k):
        for to in around:
            signal(hello.at[k], to)

    def greeted(k):
        pl.semaphore_wait(hello.at[k], 4)

    def x_copy(t, d):
        to = at.xs[d]
        source = basev if isinstance(t, int) and t == TL else pertv.at[to * TL + t]
        return pltpu.make_async_remote_copy(
            source, raw.at[t, HALO_TILES + x], xs_send, xs_recv.at[t],
            device_id={"x": to}, device_id_type=MESH,
        )

    for t in range(TL + 1):
        for d in order:
            x_copy(t, d).start()
    greet(0)
    for t in range(TL):
        raw[t, HALO_TILES + x] = pertv[x * TL + t]
    raw[TL, HALO_TILES + x] = basev[...]

    def up(t):
        buf = raw.at[t]
        return pltpu.make_async_remote_copy(
            buf.at[pl.ds(X, 2)], buf.at[pl.ds(0, 2)], y_send.at[0], y_recv.at[t, 0],
            device_id={"y": y + 1}, device_id_type=MESH,
        )

    def down(t):
        buf = raw.at[t]
        return pltpu.make_async_remote_copy(
            buf.at[pl.ds(2, 2)], buf.at[pl.ds(X + 2, 2)], y_send.at[1], y_recv.at[t, 1],
            device_id={"y": y - 1}, device_id_type=MESH,
        )

    def arrive_x(t):
        settle(raw.at[t, pl.ds(0, X - 1)], xs_recv.at[t])

    def pass_on(t):
        @pl.when(above)
        def _():
            up(t).start()

        @pl.when(below)
        def _():
            down(t).start()

    def arrive_y(t):
        buf = raw.at[t]

        @pl.when(below)
        def _():
            up(t).wait_recv()

        @pl.when(above)
        def _():
            down(t).wait_recv()

        @pl.when(jnp.logical_not(below))
        def _():
            buf[0:2] = jnp.zeros((2, 64, 128), F32)

        @pl.when(jnp.logical_not(above))
        def _():
            buf[X + 2 : X + 4] = jnp.zeros((2, 64, 128), F32)

    def rows_of(buf, row):
        return buf[row // 8, pl.ds(row % 8, 8, stride=8), :]

    for k in range(rounds - 2):
        greeted(k)
        greet(k + 1)
    arrive_x(0)
    pass_on(0)
    greeted(rounds - 2)
    greet(rounds - 1)
    arrive_x(1)
    pass_on(1)

    def spot(t):
        return got.at[t, pl.ds(pl.multiple_of(4 * me, 4), 4), :]

    def cells(t, xx, zz, cc):
        return send.at[t, xx, zz, pl.ds(pl.multiple_of(4 * cc, 4), 4), :]

    def one(t, carry):
        arrive_y(t)
        for row in range(first - 12, last + 12):
            v[row] = rows_of(raw.at[t], row)
        advance(v, w1, w2, first, last, low, high)

        @pl.when(t == 0)
        def _():
            greeted(rounds - 1)

        @pl.when(t < TL)
        def _():
            for i in range(X):
                send[t, i] = v[first + 8 * i : first + 8 * i + 8]
            pltpu.make_async_copy(cells(t, x, z, c), spot(t), a_recv.at[t]).start()
            for dz, dc, dx in at.all:
                zz, cc, xx = at.zs[dz], at.cs[dc], at.xs[dx]
                pltpu.make_async_remote_copy(
                    cells(t, xx, zz, cc), spot(t), a_send, a_recv.at[t],
                    device_id={"x": xx, "z": zz, "c": cc}, device_id_type=MESH,
                ).start()

        @pl.when(t + 2 < TL + 1)
        def _():
            arrive_x(t + 2)
            pass_on(t + 2)

        return carry

    lax.fori_loop(0, TL + 1, one, 0)

    def finish():
        settle(raw.at[:, pl.ds(0, X - 1)], xs_send)

        @pl.when(above)
        def _():
            settle(raw.at[:, pl.ds(0, 2)], y_send.at[0])

        @pl.when(below)
        def _():
            settle(raw.at[:, pl.ds(0, 2)], y_send.at[1])

        settle(got.at[:, pl.ds(0, 4 * NS - 4)], a_send)

    return finish


def inverse_factor(gram):
    row = lax.broadcasted_iota(jnp.int32, (16, 128), 0)
    lane = lax.broadcasted_iota(jnp.int32, (16, 128), 1)
    a = jnp.where(lane < 16, gram, jnp.where(lane == row + 16, 1.0, 0.0))
    def wide(col):
        return jnp.broadcast_to(col, (16, 128))

    for k in range(0, 14, 2):
        p0, p1 = wide(a[k : k + 1, :]), wide(a[k + 1 : k + 2, :])
        f0, f1 = wide(a[:, k : k + 1]), wide(a[:, k + 1 : k + 2])
        u, v, w = wide(p0[:, k : k + 1]), wide(p0[:, k + 1 : k + 2]), wide(p1[:, k + 1 : k + 2])
        scale = 1.0 / (u * w - v * v)
        change = ((f0 * w - f1 * v) * scale) * p0 + ((f1 * u - f0 * v) * scale) * p1
        a = jnp.where(row > k + 1, a - change, a)
    before = pltpu.roll(a, 1, 0)
    cross = jnp.sum(jnp.where(lane == row - 1, a, 0.0), axis=1, keepdims=True)
    first = jnp.sum(jnp.where(lane == row - 1, before, 0.0), axis=1, keepdims=True)
    odd = lax.rem(row, 2) == 1
    a = jnp.where(odd, a - cross / first * before, a)
    diagonal = jnp.sum(jnp.where(lane == row, a, 0.0), axis=1, keepdims=True)
    return a * (1.0 / jnp.sqrt(diagonal))


def reduce_body(at, finish, omega_ref, out_ref, got, v, a_recv, S, turned, wsend, wrecv, own, own_row, plane_recv, w_all, psend, pall, small, small_plane, small_column, omega, omega_sem, sends, recvs, p_recv):
    X, Y, Z, C = at.dims
    TL = got.shape[0]
    NS = X * Z * C
    cells = Y * X * 8 * 1024
    x, y, z, c = at.x, at.y, at.z, at.c
    mine, here = z * C + c, y * X + x

    def dot(a, b, dims):
        return lax.dot_general(a, b, (dims, ((), ())), precision=lax.Precision.HIGHEST, preferred_element_type=F32)

    pltpu.make_async_copy(omega_ref, omega, omega_sem).wait()
    column = lax.broadcasted_iota(jnp.int32, (X * Z * C * TL, NS), 1)
    sketch_row = lax.broadcasted_iota(jnp.int32, (X * Z * C * TL, NS), 0)
    omegas = [
        dot(omega[...], jnp.where(sketch_row == column * TL + t, 1.0, 0.0), ((1,), (0,))) for t in range(TL)
    ]
    base_row = 8 * HALO_TILES + 8 * x + z
    base = [v[base_row, pl.ds(4 * c + q, 1), :] for q in range(4)]
    sketched = jnp.zeros((16, 512), F32)
    for t in range(TL):
        everything = got.at[t]
        pltpu.make_async_copy(everything, everything, a_recv.at[t]).wait()
        snaps = [got[t, pl.ds(q, NS, stride=4), :] - base[q] for q in range(4)]
        for q in range(4):
            S[q, NS * t : NS * t + NS] = snaps[q]
            turned[t, 128 * q : 128 * q + 128] = snaps[q].T
        sketched = sketched + dot(omegas[t], jnp.concatenate(snaps, axis=1), ((1,), (0,)))
    mat = jnp.concatenate([S[q] for q in range(4)], axis=1)
    across = jnp.concatenate([turned[t] for t in range(TL)], axis=1)
    part = dot(sketched, across, ((1,), (0,))) * (1.0 / cells)
    for h in range(2):
        wsend[h] = part[:, 128 * h : 128 * h + 128]

    def remote(src, dst, k, to, recv=None):
        return pltpu.make_async_remote_copy(
            src, dst, sends.at[k], recvs.at[k] if recv is None else recv, device_id=to, device_id_type=MESH
        )

    def over_column(k, src, dst):
        for dz, dc in at.column:
            to = {"z": at.zs[dz], "c": at.cs[dc]}
            remote(src(to["z"] * C + to["c"]), dst, k, to).start()

    def over_plane(k, src, dst):
        for dy, dx in at.plane:
            remote(src, dst, k, {"y": at.ys[dy], "x": at.xs[dx]}).start()

    def arrived(k, like):
        settle(like, recvs.at[k])

    def sent(k, like):
        settle(like, sends.at[k])

    strips = wrecv.at[:, pl.ds(0, Z * C - 1), :]
    in_plane = plane_recv.at[pl.ds(0, X * Y - 1)]
    in_column = small_column.at[pl.ds(0, Z * C - 1)]
    across_z = pall.at[pl.ds(0, 4), :, pl.ds(0, Z - 1), :]

    over_column(0, lambda row: wsend.at[:, pl.ds(row, 1), :], wrecv.at[:, pl.ds(mine, 1), :])
    wrecv[:, pl.ds(mine, 1), :] = wsend[:, pl.ds(mine, 1), :]
    finish()
    arrived(0, strips)
    value = jnp.sum(wrecv[...], axis=1)
    own[...] = value
    over_plane(1, own, plane_recv.at[here])
    plane_recv[here] = value
    sent(0, strips)
    arrived(1, in_plane)
    value = jnp.sum(plane_recv[...], axis=0)
    for h in range(2):
        own_row[h, 0:1, :] = value[h : h + 1]
    over_column(2, lambda row: own_row.at[:, pl.ds(0, 1), :], w_all.at[:, pl.ds(mine, 1), :])
    for h in range(2):
        w_all[h, pl.ds(mine, 1), :] = value[h : h + 1]
    sent(1, in_plane)
    arrived(2, strips)
    weights = jnp.concatenate([w_all[0], w_all[1]], axis=1)
    proj = dot(weights, mat, ((1,), (0,)))

    row = lax.broadcasted_iota(jnp.int32, (16, 128), 0)
    lane = lax.broadcasted_iota(jnp.int32, (16, 128), 1)
    diagonal = lane // 16 == lax.rem(row, 8)
    wide = dot(proj, jnp.concatenate([proj] * 8, axis=0), ((1,), (1,))) * (1.0 / cells)
    wide = jnp.where(diagonal, wide, 0.0)
    value = jnp.concatenate([jnp.sum(wide[8 * h : 8 * h + 8], axis=0, keepdims=True) for h in range(2)], axis=0)
    small[0] = value
    over_column(3, lambda row: small.at[0], small_column.at[mine])
    small_column[mine] = value

    for q in range(4):
        psend[q] = proj[:, 128 * q : 128 * q + 128]

    def strip(core, dz):
        return pall.at[pl.ds(4 * core, 4), :, at.zs[dz], :]

    other = {"c": at.cs[1]}
    z_order = far_first(Z)[:-1]
    projected = [remote(psend, strip(c, 0), 4, {"z": at.zs[dz]}, p_recv.at[dz]) for dz in z_order]
    for copy in projected:
        copy.start()
    remote(psend, strip(c, 0), 5, other).start()
    own_p = pltpu.make_async_copy(psend, strip(c, 0), p_recv.at[0])
    own_p.start()
    sent(2, strips)
    arrived(3, in_column)
    value = jnp.sum(small_column[...], axis=0)
    small[1] = value
    over_plane(6, small.at[1], small_plane.at[here])
    small_plane[here] = value
    for copy, dz in reversed(list(zip(projected, z_order))):
        copy.wait_recv()
        back = (Z - dz) % Z
        remote(strip(c, back), strip(c, back), 5, other).start()
    sent(3, in_column)
    sent(4, across_z)
    arrived(6, in_plane)
    value = jnp.sum(small_plane[...], axis=0)
    gram = jnp.concatenate([jnp.broadcast_to(value[h : h + 1], (8, 128)) for h in range(2)], axis=0)
    gram = jnp.where(diagonal, gram, 0.0)
    for shift in (64, 32, 16):
        gram = gram + pltpu.roll(gram, shift, 1)
    inverse = inverse_factor(gram)

    own_p.wait()
    sent(6, in_plane)
    sent(5, pall.at[pl.ds(0, 4)])
    arrived(5, pall.at[pl.ds(0, 4)])
    for i in range(16):
        total = inverse[i : i + 1, 16:17] * pall[:, 0]
        for m in range(1, i + 1):
            total = total + inverse[i : i + 1, 16 + m : 17 + m] * pall[:, m]
        out_ref[i] = total


def whole_body(dims, base_ref, pert_ref, omega_ref, out_ref, got, *scratch):
    one, two = scratch[:15], scratch[15:]
    at = Places(dims)
    pltpu.make_async_copy(omega_ref, scratch[-5], scratch[-4]).start()
    finish = snapshots_body(at, base_ref, pert_ref, got, *one)
    reduce_body(at, finish, omega_ref, out_ref, got, one[3], one[-1], *two)


def basis_of(base, pert, omega, dims):
    X, Y, Z, C = dims
    TL = pert.shape[0] // X
    NS, NZC, NXY = X * Z * C, Z * C, X * Y
    rows = 8 * (X + 2 * HALO_TILES)
    sem = pltpu.SemaphoreType.DMA
    anywhere = pl.BlockSpec(memory_space=pl.ANY)
    inside = pl.BlockSpec(memory_space=pltpu.VMEM)
    vmem = lambda *shape: pltpu.VMEM(shape, F32)
    return pl.pallas_call(
        functools.partial(whole_body, dims),
        out_shape=pltpu.VMEM((16, 8, 8, 128), F32),
        in_specs=[anywhere] * 3,
        out_specs=inside,
        scratch_shapes=[
            vmem(TL, NS * 4, 128),
            vmem(X * TL, 64, 128),
            vmem(64, 128),
            vmem(TL + 1, rows // 8, 64, 128),
            vmem(rows, 8, 128),
            vmem(rows, 8, 128),
            vmem(rows, 8, 128),
            vmem(TL, X, Z, 8, 128),
            sem((2,)),
            pltpu.SemaphoreType.REGULAR((max(Z, Y) // 2,)),
            sem,
            sem((TL + 1,)),
            sem((2,)),
            sem((TL + 1, 2)),
            sem,
            sem((TL,)),
            vmem(4, NS * TL, 128),
            vmem(TL, 512, NS),
            vmem(2, 16, 128),
            vmem(2, 16, 128),
            vmem(2, 128),
            vmem(2, 8, 128),
            vmem(NXY, 2, 128),
            vmem(2, 16, 128),
            vmem(4, 16, 128),
            vmem(8, 16, 8, 128),
            vmem(2, 2, 128),
            vmem(NXY, 2, 128),
            vmem(NZC, 2, 128),
            vmem(16, NS * TL),
            sem,
            sem((7,)),
            sem((7,)),
            sem((Z,)),
        ],
        compiler_params=pltpu.CompilerParams(collective_id=0, has_side_effects=True),
    )(base, pert, omega)


def tiles_first(a):
    lead = a.shape[:-2]
    a = a.reshape(*lead, 8, 8, 128)
    n = len(lead)
    return a.transpose(*range(n), n + 1, n, n + 2).reshape(*lead, 64, 128)


def body(dims, base_state, perturbations, sketch):
    out = basis_of(tiles_first(base_state), tiles_first(perturbations[0]), sketch.T, dims)
    return out.transpose(0, 2, 1, 3).reshape(16, 8, 1024)


def solution(mesh, along_x=ALONG_X):
    traj, space = mesh.shape["traj"], mesh.shape["space"]
    dims = (along_x, space // along_x, traj // CORES, CORES)
    X, Y, Z, C = dims
    torus = Mesh(mesh.devices.reshape(Z, C, Y, X), ("z", "c", "y", "x"))
    return jax.shard_map(
        functools.partial(body, dims),
        mesh=torus,
        in_specs=(P(("y", "x"), None), P(("z", "c"), None, ("y", "x"), None), P()),
        out_specs=P(None, ("y", "x"), None),
        check_vma=False,
    )
```

time: 86.9 us -> 66.1 us (0.76)
  Pallas kernels: 84.7 us -> 65.2 us
  local copies, waits for them, and re-layouts: 1.89 us -> 0.8 us
    pallas_call x1, Pallas kernels: 84.7 us -> 65.2 us  [basis_of(): pl.pallas_call(functools.partial(whole_body, dims), out_shape=pltpu.VMEM(...]
    unnamed x1, local copies, waits for them, and re-layouts: 1.89 us -> 0.8 us
where the time goes in v2:
time: 66.1 us; the launch traced here: 66 us
  Pallas kernels  65.2 us (99%)
  local copies, waits for them, and re-layouts  0.8 us (1%)
    pallas_call x1, Pallas kernels, basis_of(): pl.pallas_call(functools.partial(whole_body, dims), out_shape=pltpu.VMEM(...  65.2 us

profile of v2, /device:TPU:1, one launch (start us, length us, event | category | flops | bytes accessed | tf_op | source)
XLA Modules:
  0.0 66.0 jit_solution(17913669184811845408)
XLA Ops:
  0.0 65.2 %shard_map.37 = f32[16,8,8,128]{3,2,1,0:T(8,128)S(1)} custom-call(f32[64,128]{1,0:T(8,128)} %bitcast.16, f32[16,64,128]{2,1,0:T(8,128)} %bitcast.15, f32[16,256]{1,0:T(8,128)} %bitcast.17), custom_call_target="tpu_custom_call" | custom-call | tf_op jit(solution)/shard_map/pallas_call | solution.py:443
  65.2 0.8 %copy.5 = f32[16,8,1024]{2,1,0:T(8,128)} copy(f32[16,8,1024]{2,1,0:T(8,128)S(1)} %bitcast.14) | data formatting | bytes 1048576

commit v3 on v2

--- a/solution.py
+++ b/solution.py
@@ -90,9 +90,14 @@
             ((dy, dx) for dy in range(Y) for dx in range(X) if dy or dx),
             key=lambda d: -min(d[0], Y - d[0]) - min(d[1], X - d[1]),
         )
+        self.ring = [(dc, dx) for dx in far_first(X) for dc in range(C) if dc or dx]
+        self.sheet = sorted(
+            ((dz, dy) for dz in range(Z) for dy in range(Y) if dz or dy),
+            key=lambda d: -min(d[0], Z - d[0]) - min(d[1], Y - d[1]),
+        )
         self.all = sorted(
             ((dz, dc, dx) for dz in range(Z) for dc in range(C) for dx in range(X) if dz or dc or dx),
-            key=lambda d: -min(d[0], Z - d[0]) - min(d[2], X - d[2]),
+            key=lambda d: (-min(d[0], Z - d[0]), d[1], -min(d[2], X - d[2]), d[2], d[0]),
         )
 
 
@@ -146,9 +151,11 @@
             device_id={"x": to}, device_id_type=MESH,
         )
 
-    for t in range(TL + 1):
+    def give_x(t):
         for d in order:
             x_copy(t, d).start()
+
+    give_x(0)
     greet(0)
     for t in range(TL):
         raw[t, HALO_TILES + x] = pertv[x * TL + t]
@@ -205,12 +212,18 @@
     for k in range(rounds - 2):
         greeted(k)
         greet(k + 1)
+        if k + 1 < TL - 1:
+            give_x(k + 1)
+    for t in range(rounds - 1, TL - 1):
+        give_x(t)
     arrive_x(0)
     pass_on(0)
+    give_x(TL - 1)
     greeted(rounds - 2)
     greet(rounds - 1)
     arrive_x(1)
     pass_on(1)
+    give_x(TL)
 
     def spot(t):
         return got.at[t, pl.ds(pl.multiple_of(4 * me, 4), 4), :]
@@ -220,6 +233,12 @@
 
     def one(t, carry):
         arrive_y(t)
+
+        @pl.when(t + 2 < TL + 1)
+        def _():
+            arrive_x(t + 2)
+            pass_on(t + 2)
+
         for row in range(first - 12, last + 12):
             v[row] = rows_of(raw.at[t], row)
         advance(v, w1, w2, first, last, low, high)
@@ -239,11 +258,6 @@
                     cells(t, xx, zz, cc), spot(t), a_send, a_recv.at[t],
                     device_id={"x": xx, "z": zz, "c": cc}, device_id_type=MESH,
                 ).start()
-
-        @pl.when(t + 2 < TL + 1)
-        def _():
-            arrive_x(t + 2)
-            pass_on(t + 2)
 
         return carry
 
@@ -288,7 +302,7 @@
     return a * (1.0 / jnp.sqrt(diagonal))
 
 
-def reduce_body(at, finish, omega_ref, out_ref, got, v, a_recv, S, turned, wsend, wrecv, own, own_row, plane_recv, w_all, psend, pall, small, small_plane, small_column, omega, omega_sem, sends, recvs, p_recv):
+def reduce_body(at, finish, omega_ref, out_ref, got, v, a_recv, S, turned, wsend, wrecv, own, own_row, sheet_recv, w_all, psend, pall, small, small_plane, small_column, omega, omega_sem, sends, recvs, p_recv):
     X, Y, Z, C = at.dims
     TL = got.shape[0]
     NS = X * Z * C
@@ -342,29 +356,39 @@
     def sent(k, like):
         settle(like, sends.at[k])
 
-    strips = wrecv.at[:, pl.ds(0, Z * C - 1), :]
-    in_plane = plane_recv.at[pl.ds(0, X * Y - 1)]
+    in_ring = wrecv.at[pl.ds(0, X * C - 1)]
+    in_sheet = sheet_recv.at[pl.ds(0, Z * Y - 1)]
+    in_plane = small_plane.at[pl.ds(0, X * Y - 1)]
     in_column = small_column.at[pl.ds(0, Z * C - 1)]
     across_z = pall.at[pl.ds(0, 4), :, pl.ds(0, Z - 1), :]
 
-    over_column(0, lambda row: wsend.at[:, pl.ds(row, 1), :], wrecv.at[:, pl.ds(mine, 1), :])
-    wrecv[:, pl.ds(mine, 1), :] = wsend[:, pl.ds(mine, 1), :]
+    share = 16 // (X * C)
+    part_of = c * X + x
+    for dc, dx in at.ring:
+        to = {"c": at.cs[dc], "x": at.xs[dx]}
+        theirs = pl.ds(share * (to["c"] * X + to["x"]), share)
+        remote(wsend.at[:, theirs, :], wrecv.at[part_of], 0, to).start()
+    wrecv[part_of] = wsend[:, pl.ds(share * part_of, share), :]
     finish()
-    arrived(0, strips)
-    value = jnp.sum(wrecv[...], axis=1)
+    arrived(0, in_ring)
+    value = jnp.sum(wrecv[...], axis=0)
     own[...] = value
-    over_plane(1, own, plane_recv.at[here])
-    plane_recv[here] = value
-    sent(0, strips)
-    arrived(1, in_plane)
-    value = jnp.sum(plane_recv[...], axis=0)
+    for dz, dy in at.sheet:
+        remote(own, sheet_recv.at[z * Y + y], 1, {"z": at.zs[dz], "y": at.ys[dy]}).start()
+    sheet_recv[z * Y + y] = value
+    sent(0, in_ring)
+    arrived(1, in_sheet)
+    value = jnp.sum(sheet_recv[...], axis=0)
     for h in range(2):
-        own_row[h, 0:1, :] = value[h : h + 1]
-    over_column(2, lambda row: own_row.at[:, pl.ds(0, 1), :], w_all.at[:, pl.ds(mine, 1), :])
+        own_row[h, 0:share, :] = value[h]
+    mine_rows = pl.ds(share * part_of, share)
+    for dc, dx in at.ring:
+        to = {"c": at.cs[dc], "x": at.xs[dx]}
+        remote(own_row.at[:, pl.ds(0, share), :], w_all.at[:, mine_rows, :], 2, to).start()
     for h in range(2):
-        w_all[h, pl.ds(mine, 1), :] = value[h : h + 1]
-    sent(1, in_plane)
-    arrived(2, strips)
+        w_all[h, mine_rows, :] = value[h]
+    sent(1, in_sheet)
+    arrived(2, in_ring)
     weights = jnp.concatenate([w_all[0], w_all[1]], axis=1)
     proj = dot(weights, mat, ((1,), (0,)))
 
@@ -387,12 +411,13 @@
     other = {"c": at.cs[1]}
     z_order = far_first(Z)[:-1]
     projected = [remote(psend, strip(c, 0), 4, {"z": at.zs[dz]}, p_recv.at[dz]) for dz in z_order]
+    sent(2, in_ring)
+    sent(3, in_column)
     for copy in projected:
         copy.start()
     remote(psend, strip(c, 0), 5, other).start()
     own_p = pltpu.make_async_copy(psend, strip(c, 0), p_recv.at[0])
     own_p.start()
-    sent(2, strips)
     arrived(3, in_column)
     value = jnp.sum(small_column[...], axis=0)
     small[1] = value
@@ -402,7 +427,6 @@
         copy.wait_recv()
         back = (Z - dz) % Z
         remote(strip(c, back), strip(c, back), 5, other).start()
-    sent(3, in_column)
     sent(4, across_z)
     arrived(6, in_plane)
     value = jnp.sum(small_plane[...], axis=0)
@@ -465,10 +489,10 @@
             vmem(4, NS * TL, 128),
             vmem(TL, 512, NS),
             vmem(2, 16, 128),
-            vmem(2, 16, 128),
-            vmem(2, 128),
+            vmem(X * C, 2, 16 // (X * C), 128),
+            vmem(2, 16 // (X * C), 128),
             vmem(2, 8, 128),
-            vmem(NXY, 2, 128),
+            vmem(Z * Y, 2, 16 // (X * C), 128),
             vmem(2, 16, 128),
             vmem(4, 16, 128),
             vmem(8, 16, 8, 128),

time: 66.1 us -> 65.8 us (level)
  no operation moved by 1% of the time
where the time goes in v3:
time: 65.8 us; the launch traced here: 65.7 us
  Pallas kernels  64.9 us (99%)
  local copies, waits for them, and re-layouts  0.8 us (1%)
    pallas_call x1, Pallas kernels, basis_of(): pl.pallas_call(functools.partial(whole_body, dims), out_shape=pltpu.VMEM(...  64.9 us

profile of v3, /device:TPU:1, one launch (start us, length us, event | category | flops | bytes accessed | tf_op | source)
XLA Modules:
  0.0 65.7 jit_solution(7074666331535380185)
XLA Ops:
  0.0 64.9 %shard_map.37 = f32[16,8,8,128]{3,2,1,0:T(8,128)S(1)} custom-call(f32[64,128]{1,0:T(8,128)} %bitcast.16, f32[16,64,128]{2,1,0:T(8,128)} %bitcast.15, f32[16,256]{1,0:T(8,128)} %bitcast.17), custom_call_target="tpu_custom_call" | custom-call | tf_op jit(solution)/shard_map/pallas_call | solution.py:467
  64.9 0.8 %copy.5 = f32[16,8,1024]{2,1,0:T(8,128)} copy(f32[16,8,1024]{2,1,0:T(8,128)S(1)} %bitcast.14) | data formatting | bytes 1048576

commit v4 on v3

--- a/solution.py
+++ b/solution.py
@@ -33,7 +33,7 @@
         if at < first:
             at = min(first, hi)
         elif at < last:
-            at = min(at + 8, last)
+            at = min(at + 4, last)
         else:
             at = hi
         cuts.append(at)
@@ -232,13 +232,12 @@
         return send.at[t, xx, zz, pl.ds(pl.multiple_of(4 * cc, 4), 4), :]
 
     def one(t, carry):
-        arrive_y(t)
-
         @pl.when(t + 2 < TL + 1)
         def _():
             arrive_x(t + 2)
             pass_on(t + 2)
 
+        arrive_y(t)
         for row in range(first - 12, last + 12):
             v[row] = rows_of(raw.at[t], row)
         advance(v, w1, w2, first, last, low, high)

time: 65.8 us -> 65.8 us (level)
  no operation moved by 1% of the time
where the time goes in v4:
time: 65.8 us; the launch traced here: 65.7 us
  Pallas kernels  64.8 us (98%)
  local copies, waits for them, and re-layouts  0.8 us (1%)
    pallas_call x1, Pallas kernels, basis_of(): pl.pallas_call(functools.partial(whole_body, dims), out_shape=pltpu.VMEM(...  64.8 us

profile of v4, /device:TPU:1, one launch (start us, length us, event | category | flops | bytes accessed | tf_op | source)
XLA Modules:
  0.0 65.7 jit_solution(13606329040324996602)
XLA Ops:
  0.0 64.8 %shard_map.37 = f32[16,8,8,128]{3,2,1,0:T(8,128)S(1)} custom-call(f32[64,128]{1,0:T(8,128)} %bitcast.16, f32[16,64,128]{2,1,0:T(8,128)} %bitcast.15, f32[16,256]{1,0:T(8,128)} %bitcast.17), custom_call_target="tpu_custom_call" | custom-call | tf_op jit(solution)/shard_map/pallas_call | solution.py:466
  64.9 0.8 %copy.5 = f32[16,8,1024]{2,1,0:T(8,128)} copy(f32[16,8,1024]{2,1,0:T(8,128)S(1)} %bitcast.14) | data formatting | bytes 1048576
